TPU v7x, 32 devices: a whole 2x2x4 slice. The times are simulated.
32 devices in a mesh: dp: 16 (over z, x, core), rep: 2 (over y).
Axes of the slice: x: 2, y: 2, z: 4, core: 2. Of those that a mesh axis runs over, the one named last changes fastest.
Arguments:
- grad_out: bfloat16 [12288, 2048], P('dp', 'rep'), may hold values from -6 to 6
- pre_act: bfloat16 [12288, 3072], P('dp', 'rep'), may hold values from -6 to 6
- up_weight: bfloat16 [3072, 2048], P('rep'), may hold values from -0.125 to 0.125
- down_weight: bfloat16 [2048, 3072], P(None, 'rep'), may hold values from -0.109375 to 0.109375
- slot_counts: int32 [16], P('dp'), may hold values from 384 to 768, as said below
Outputs:
- input_grad: bfloat16 [12288, 2048], P('dp')
- down_grad: float32 [2048, 3072], P('dp', 'rep')
Inputs may be any that keep to these rules, and one draw needn't show every extreme that they name: Row i * 768 + j is live exactly when j < slot_counts[i]; some index has all 768 slots live and some index exactly 384.
All inputs are finite; a program needn't handle non-finite values.
Results may differ from a plain program's by a relative error of at most 0.0049.
Values may be sent and summed in bfloat16 or wider, within the bound.
A program may use at most 128 MiB of HBM per device.

v0:
```python
import jax
import jax.numpy as jnp
from jax import lax
from jax.sharding import PartitionSpec as P


def on_device(grad_out, pre_act, up_weight, down_weight, slot_counts):
    slot_rows = grad_out.shape[0]
    live_rows = (lax.iota(jnp.int32, slot_rows) < slot_counts[0])[:, None]
    grad_full = lax.all_gather(grad_out, "rep", axis=1, tiled=True)
    grad_live = jnp.where(live_rows, grad_full, jnp.zeros_like(grad_full))
    zero_pre = jnp.zeros_like(pre_act)
    hidden = jnp.where(live_rows, jnp.maximum(pre_act, zero_pre), zero_pre)
    data_ranks = lax.axis_size("dp")
    down_sum = lax.psum_scatter(
        lax.dot_general(
            grad_live, hidden, (((0,), (0,)), ((), ())), preferred_element_type=jnp.float32
        ),
        "dp",
        scatter_dimension=0,
        tiled=True,
    )
    down_grad = down_sum / data_ranks
    hidden_grad = jnp.dot(grad_live, down_weight, preferred_element_type=jnp.float32)
    pre_grad = jnp.where(pre_act > 0, hidden_grad, jnp.zeros_like(hidden_grad)).astype(jnp.bfloat16)
    partial_terms = jnp.dot(pre_grad, up_weight, preferred_element_type=jnp.float32)
    input_sum = lax.psum(partial_terms, "rep")
    input_grad = input_sum.astype(jnp.bfloat16)
    return (input_grad, down_grad)


def solution(mesh):
    return jax.shard_map(
        on_device,
        mesh=mesh,
        in_specs=(P("dp", "rep"), P("dp", "rep"), P("rep", None), P(None, "rep"), P("dp")),
        out_specs=(P("dp", None), P("dp", "rep")),
        check_vma=False,
    )
```

profile of v0, /device:TPU:0, one launch (start us, length us, event | category | flops | bytes accessed | tf_op | source)
XLA Modules:
  0.0 245.0 jit_solution(6977455939318011038)
XLA Ops:
  7.2 0.0 all-gather.2.cloned.1.call-start
  7.2 0.7 all-gather.2.cloned.1.call-update
  7.9 0.0 reduce-scatter.2.cloned.1.call-start
  8.6 48.6 %all-gather.2.cloned.1.call-done = bf16[768,2048]{1,0:T(8,128)(2,1)} async-done(((bf16[768,1024]{1,0:T(8,128)(2,1)}), bf16[768,2048]{1,0:T(8,128)(2,1)}) %all-gather.2.cloned.1.call-update) | async-done | bytes 3145744 | tf_op jit(solution)/shard_map/all_gather | solution.py:10
  57.2 10.7 %fusion = f32[2048,1536]{1,0:T(8,128)} fusion(bf16[768,1536]{1,0:T(8,128)(2,1)} %param.6, pred[768]{0:T(1024)(128)(4,1)S(1)} %iota_compare_fusion, bf16[768,2048]{1,0:T(8,128)(2,1)} %all-gather.2.cloned.1.call-done), kind=kOutput, calls=%fused_computation.2 | convolution fusion | flops 4835770368 | bytes 18088704 | tf_op jit(solution)/shard_map/dot_general | solution.py:16
  67.9 0.0 copy-start
  67.9 0.0 reduce-scatter.2.cloned.1.call-update
  67.9 1.9 copy-done
  69.8 19.0 %fusion.5 = f32[768,2048]{1,0:T(8,128)} fusion(bf16[1536,2048]{1,0:T(8,128)(2,1)} %param.7, bf16[768,1536]{1,0:T(8,128)(2,1)} %param.6, bf16[2048,1536]{1,0:T(8,128)(2,1)} %param.8, bf16[768,2048]{1,0:T(8,128)(2,1)S(1)} %copy-done, pred[768]{0:T(1024)(128)(4,1)S(1)} %iota_compare_fusion), kind=kOutput, calls=%fused_computation.7 | convolution fusion | flops 9668788224 | bytes 24380160 | tf_op jit(solution)/shard_map/dot_general | solution.py:26
  88.8 147.3 %all-reduce.1 = bf16[768,2048]{1,0:T(8,128)(2,1)} all-reduce(f32[768,2048]{1,0:T(8,128)} %fusion.5), channel_id=1, replica_groups=mesh['dp'=16,'rep'=2] {'rep'}, use_global_device_ids=true, to_apply=%region_0.1 | all-reduce | flops 1572864 | bytes 9437184 | tf_op jit(solution)/shard_map/psum | solution.py:27
  236.1 0.0 reduce-scatter.2.cloned.1.call-done
  236.1 2.1 broadcast_multiply_fusion
  (1 shorter events, 0.0 us)
Async XLA Ops:
  7.2 50.0 %all-gather.2.cloned.1.call-start = ((), (), s32[]{:S(2)}) async-start(), calls=%async_computation.1 | async-start | bytes 4718592 | tf_op jit(solution)/shard_map/all_gather | solution.py:10
  7.9 228.2 %reduce-scatter.2.cloned.1.call-start = ((), (), s32[]{:S(2)}) async-start(), calls=%async_computation.2 | async-start | bytes 13369344 | tf_op jit(solution)/shard_map/reduce_scatter | solution.py:15
  67.9 1.9 copy-start
Sparse Core Ops, SparseCore 0:
  9.5 47.6 all-gather.1
  68.1 134.9 reduce-scatter.1
where the time goes:
time: 245 us
  blocking collectives  147 us (60%)
  waiting for transfers between devices  49.3 us (20%)
  matrix products  29.7 us (12%)
  between operations  14.7 us (6%)
    psum x1, blocking collectives, on_device(): input_sum = lax.psum(partial_terms, 'rep')  147 us
    all_gather x1, waiting for transfers between devices, on_device(): grad_full = lax.all_gather(grad_out, 'rep', axis=1, tiled=True)  48.6 us
    dot_general x1, matrix products, on_device(): jnp.dot(pre_grad, up_weight, preferred_element_type=jnp.float32)  19 us
    dot_general x1, matrix products, on_device(): lax.dot_general(grad_live, hidden, (((0,), (0,)), ((), ())), preferred_el...  10.7 us
  transfers between devices with their start and end apart: 2, of which 1 were waited for; matrix products, arithmetic and copies ran while one was open for 8% of the time, Pallas kernels for 0%

commit v1 on v0

--- a/solution.py
+++ b/solution.py
@@ -24,7 +24,7 @@
     hidden_grad = jnp.dot(grad_live, down_weight, preferred_element_type=jnp.float32)
     pre_grad = jnp.where(pre_act > 0, hidden_grad, jnp.zeros_like(hidden_grad)).astype(jnp.bfloat16)
     partial_terms = jnp.dot(pre_grad, up_weight, preferred_element_type=jnp.float32)
-    input_sum = lax.psum(partial_terms, "rep")
+    input_sum = jnp.sum(lax.all_gather(partial_terms, "rep"), axis=0)
     input_grad = input_sum.astype(jnp.bfloat16)
     return (input_grad, down_grad)
 

time: 245 us -> 377 us (1.54)
  waiting for transfers between devices: 49.3 us -> 319 us
  blocking collectives: 147 us -> 0 us
  other arithmetic: 2.08 us -> 10.6 us
    psum x1 -> x0, blocking collectives: 147 us -> none  [on_device(): input_sum = lax.psum(partial_terms, 'rep')]
    all_gather x0 -> x1, waiting for transfers between devices: none -> 139 us  [on_device(): input_sum = jnp.sum(lax.all_gather(partial_terms, 'rep'), axis=0)]
    reduce_scatter x1, waiting for transfers between devices: 0.01 us -> 131 us  [on_device(): lax.psum_scatter(lax.dot_general(grad_live, hidden, (((0,), (0,)), ((), (...]
    reduce_sum x0 -> x1, other arithmetic: none -> 8.5 us  [on_device(): input_sum = jnp.sum(lax.all_gather(partial_terms, 'rep'), axis=0)]
  transfers between devices with their start and end apart: 2 -> 3, of which waited for: 1 -> 3; matrix products, arithmetic and copies ran while one was open for 8% -> 5% of each run, Pallas kernels for 0% -> 0%
where the time goes in v1:
time: 377 us; the launch traced here: 376 us
  waiting for transfers between devices  319 us (85%)
  matrix products  31 us (8%)
  between operations  14.4 us (4%)
  other arithmetic  10.6 us (3%)
    all_gather x1, waiting for transfers between devices, on_device(): input_sum = jnp.sum(lax.all_gather(partial_terms, 'rep'), axis=0)  139 us
    reduce_scatter x1, waiting for transfers between devices, on_device(): lax.psum_scatter(lax.dot_general(grad_live, hidden, (((0,), (0,)), ((), (...  131 us
    all_gather x1, waiting for transfers between devices, on_device(): grad_full = lax.all_gather(grad_out, 'rep', axis=1, tiled=True)  48.6 us
    dot_general x1, matrix products, on_device(): jnp.dot(pre_grad, up_weight, preferred_element_type=jnp.float32)  19 us
    dot_general x1, matrix products, on_device(): lax.dot_general(grad_live, hidden, (((0,), (0,)), ((), ())), preferred_el...  12 us
    reduce_sum x1, other arithmetic, on_device(): input_sum = jnp.sum(lax.all_gather(partial_terms, 'rep'), axis=0)  8.5 us
  transfers between devices with their start and end apart: 3, of which 3 were waited for; matrix products, arithmetic and copies ran while one was open for 5% of the time, Pallas kernels for 0%

profile of v1, /device:TPU:0, one launch (start us, length us, event | category | flops | bytes accessed | tf_op | source)
XLA Modules:
  0.0 376.4 jit_solution(8060342732184660241)
XLA Ops:
  7.2 0.0 all-gather.4.cloned.1.call-start
  7.2 0.7 all-gather.4.cloned.1.call-update
  7.9 0.0 all-gather.6.cloned.1.call-start
  8.6 48.6 %all-gather.4.cloned.1.call-done = bf16[768,2048]{1,0:T(8,128)(2,1)} async-done(((bf16[768,1024]{1,0:T(8,128)(2,1)}), bf16[768,2048]{1,0:T(8,128)(2,1)}) %all-gather.4.cloned.1.call-update) | async-done | bytes 3145744 | tf_op jit(solution)/shard_map/all_gather | solution.py:10
  57.2 19.0 %fusion.5 = f32[768,2048]{1,0:T(8,128)} fusion(bf16[1536,2048]{1,0:T(8,128)(2,1)} %param.7, bf16[768,1536]{1,0:T(8,128)(2,1)} %param.6, bf16[2048,1536]{1,0:T(8,128)(2,1)} %param.8, bf16[768,2048]{1,0:T(8,128)(2,1)} %all-gather.4.cloned.1.call-done, pred[768]{0:T(1024)(128)(4,1)S(1)} %iota_compare_fusion), kind=kOutput, calls=%fused_computation.7 | convolution fusion | flops 9668788224 | bytes 24380160 | tf_op jit(solution)/shard_map/dot_general | solution.py:26
  76.1 0.0 copy-start
  76.1 0.0 all-gather.6.cloned.1.call-update
  76.2 0.0 reduce-scatter.2.cloned.1.call-start
  76.2 1.8 copy-done
  78.0 12.0 %fusion = f32[2048,1536]{1,0:T(8,128)} fusion(bf16[768,1536]{1,0:T(8,128)(2,1)} %param.6, pred[768]{0:T(1024)(128)(4,1)S(1)} %iota_compare_fusion, bf16[768,2048]{1,0:T(8,128)(2,1)S(1)} %copy-done), kind=kOutput, calls=%fused_computation.2 | convolution fusion | flops 4835770368 | bytes 18088704 | tf_op jit(solution)/shard_map/dot_general | solution.py:16
  90.0 0.0 reduce-scatter.2.cloned.1.call-update
  90.1 138.8 %all-gather.6.cloned.1.call-done = f32[1536,2048]{1,0:T(8,128)} async-done(((f32[768,2048]{1,0:T(8,128)}), f32[1536,2048]{1,0:T(8,128)}) %all-gather.6.cloned.1.call-update) | async-done | bytes 12582928 | tf_op jit(solution)/shard_map/all_gather | solution.py:27
  228.8 8.5 %reduce_sum.9 = bf16[768,2048]{1,0:T(8,128)(2,1)} reduce(f32[2,768,2048]{2,1,0:T(8,128)} %bitcast.5, f32[]{:T(128)} %constant.4.clone.1), dimensions={0}, to_apply=%region_0.1 | reduce | flops 1572864 | bytes 15728644 | tf_op jit(solution)/shard_map/reduce_sum | solution.py:27
  237.3 130.5 %reduce-scatter.2.cloned.1.call-done = f32[128,1536]{1,0:T(8,128)} async-done(((f32[2048,1536]{1,0:T(8,128)}), f32[128,1536]{1,0:T(8,128)}) %reduce-scatter.2.cloned.1.call-update) | async-done | bytes 786448 | tf_op jit(solution)/shard_map/reduce_scatter | solution.py:15
  367.8 2.1 broadcast_multiply_fusion
  (1 shorter events, 0.0 us)
Async XLA Ops:
  7.2 50.0 %all-gather.4.cloned.1.call-start = ((), (), s32[]{:S(2)}) async-start(), calls=%async_computation.1 | async-start | bytes 4718592 | tf_op jit(solution)/shard_map/all_gather | solution.py:10
  7.9 220.9 %all-gather.6.cloned.1.call-start = ((), (), s32[]{:S(2)}) async-start(), calls=%async_computation.3 | async-start | bytes 18874368 | tf_op jit(solution)/shard_map/all_gather | solution.py:27
  76.1 1.9 copy-start
  76.2 291.7 %reduce-scatter.2.cloned.1.call-start = ((), (), s32[]{:S(2)}) async-start(), calls=%async_computation.2 | async-start | bytes 13369344 | tf_op jit(solution)/shard_map/reduce_scatter | solution.py:15
Sparse Core Ops, SparseCore 0:
  9.5 47.6 all-gather.3
  76.3 152.4 all-gather.5
  232.9 134.9 reduce-scatter.1
